TPU v7x, 32 devices: a whole 2x2x4 slice. The times are simulated.
32 devices in a mesh: space: 8 (over y, x, core), mode: 4 (over z).
Axes of the slice: x: 2, y: 2, z: 4, core: 2. Of those that a mesh axis runs over, the one named last changes fastest.
Arguments:
- start_modes: float32 [256, 24576], P('mode', 'space')
- hessian: bfloat16 [128, 8, 192, 192], P('space'), may hold values from -0.15625 to 0.15625
- block_exponent: int32 [128, 8], P('space'), may hold values from -1 to 1
- col_block: int32 [128, 8], P('space'), may hold values from 0 to 19, as said below
- grain_count: int32 [8], P('space'), may hold values from 384 to 512, as said below
Outputs:
- modes: float32 [256, 24576], P('mode', 'space')
Inputs may be any that keep to these rules, and one draw needn't show every extreme that they name: col_block[b, k] lies between b mod 16 and b mod 16 + 2 * 2; slot 0 is b mod 16 + 2; both ends are reached in every slab. `grain_count`: at most 512 grains a slab, reached by at least one slab.
All inputs are finite; a program needn't handle non-finite values.
Results may differ from a plain program's by a relative error of at most 0.0034.
Values may be sent and summed in bfloat16 or wider, within the bound.
A program may use at most 64 MiB of HBM per device.

v0:
```python
import jax
import jax.numpy as jnp
from jax import lax
from jax.sharding import PartitionSpec as P

HALO_BLOCKS = 2
filter_center = -0.5
filter_half = 1.5


def extended(cells, sides, width):
    for axis, dim in sides:
        count = lax.axis_size(axis)
        head = lax.slice_in_dim(cells, 0, width, axis=dim)
        tail = lax.slice_in_dim(cells, cells.shape[dim] - width, cells.shape[dim], axis=dim)
        cells = jnp.concatenate(
            [
                lax.ppermute(tail, axis, [(i, (i + 1) % count) for i in range(count)]),
                cells,
                lax.ppermute(head, axis, [((i + 1) % count, i) for i in range(count)]),
            ],
            axis=dim,
        )
    return cells


def per_device(start_modes, hessian, block_exponent, col_block, grain_count):
    panel_size, rows_here = start_modes.shape
    slab_blocks, contacts, block_size, _ = hessian.shape
    halo_width = HALO_BLOCKS * block_size
    places = lax.broadcasted_iota(jnp.int32, (rows_here,), 0)
    live = (places < 6 * grain_count[0]).astype(jnp.float32)
    scales = jnp.exp2(block_exponent.astype(jnp.float32)).astype(jnp.bfloat16)

    def operate(vectors_low):
        padded = extended(vectors_low, (("space", 1),), halo_width)
        window = padded.reshape(panel_size, slab_blocks + 2 * HALO_BLOCKS, block_size)
        gathered = jnp.take(window, col_block, axis=1)
        gathered = gathered * scales[None, :, :, None]
        image = jnp.einsum("rkij,prkj->pri", hessian, gathered, preferred_element_type=jnp.float32)
        return image.reshape(panel_size, rows_here)

    start = start_modes * live
    image = operate(start.astype(jnp.bfloat16))
    first = (image - filter_center * start) / filter_half * live
    image = operate(first.astype(jnp.bfloat16))
    second = (2.0 * (image - filter_center * first) / filter_half - start) * live
    my_index = lax.axis_index("mode")
    whole = lax.all_gather(second, "mode", axis=0, tiled=True)
    partial_rows = jnp.dot(
        second, whole.T, precision=lax.Precision.HIGHEST, preferred_element_type=jnp.float32
    )
    summed_rows = lax.psum(partial_rows, "space")
    gram = lax.all_gather(summed_rows, "mode", axis=0, tiled=True)
    lower_factor = jnp.linalg.cholesky(gram)
    identity_matrix = jnp.eye(gram.shape[0], dtype=jnp.float32)
    inverse_factor = jax.scipy.linalg.solve_triangular(lower_factor, identity_matrix, lower=True)
    own_inverse = lax.dynamic_slice_in_dim(inverse_factor, my_index * panel_size, panel_size, 0)
    return jnp.dot(
        own_inverse, whole, precision=lax.Precision.HIGHEST, preferred_element_type=jnp.float32
    )


def solution(mesh):
    return jax.shard_map(
        per_device,
        mesh=mesh,
        in_specs=(
            P("mode", "space"),
            P("space", None, None, None),
            P("space", None),
            P("space", None),
            P("space"),
        ),
        out_specs=P("mode", "space"),
        check_vma=False,
    )
```

profile of v0, /device:TPU:0, one launch (start us, length us, event | category | flops | bytes accessed | tf_op | source)
XLA Modules:
  0.0 278.4 jit_solution(5893356217424159986)
XLA Ops:
  7.2 1.2 multiply_convert_fusion
  9.0 2.9 %collective-permute-start.1 = (bf16[64,384]{1,0:T(8,128)(2,1)S(1)}, bf16[64,384]{1,0:T(8,128)(2,1)S(1)}, u32[]{:S(2)}, u32[]{:S(2)}) collective-permute-start(bf16[64,384]{1,0:T(8,128)(2,1)S(1)} %get-tuple-element.27), channel_id=1, source_target_pairs={{4,0},{8,4},{12,8},{16,12},{20,16},{24,20},{28,24},{0,28},{5,1},{9... | collective-permute-start | bytes 147464 | tf_op jit(solution)/shard_map/ppermute | solution.py:20
  15.3 2.8 gather_fusion
  18.1 11.0 %fusion.10 = f32[64,16,192]{2,0,1:T(8,128)} fusion(bf16[16,8,192,192]{3,2,1,0:T(8,128)(2,1)} %param.8, bf16[16,8,64,192]{3,2,1,0:T(8,128)(2,1)} %bitcast.60, pred[16,8]{1,0:T(8,128)(4,1)S(1)} %copy.26, bf16[16,8]{1,0:T(8,128)(2,1)S(1)} %copy.30), kind=kOutput, calls=%fused_computation.16 | convolution fusion | flops 607125504 | bytes 13369728 | tf_op jit(solution)/shard_map/rkij,prkj->pri/dot_general | solution.py:40
  29.1 1.9 copy.31
  32.3 1.9 collective-permute-start.3
  34.2 1.8 collective-permute-done.2
  36.8 1.9 reshape.46
  38.9 2.8 gather_fusion.1
  41.6 11.0 %fusion.11 = f32[64,16,192]{2,0,1:T(8,128)} fusion(bf16[16,8,192,192]{3,2,1,0:T(8,128)(2,1)} %param.8, bf16[16,8,64,192]{3,2,1,0:T(8,128)(2,1)} %bitcast.59, pred[16,8]{1,0:T(8,128)(4,1)S(1)} %copy.26, bf16[16,8]{1,0:T(8,128)(2,1)S(1)} %copy.30), kind=kOutput, calls=%fused_computation.17 | convolution fusion | flops 607125504 | bytes 13369728 | tf_op jit(solution)/shard_map/rkij,prkj->pri/dot_general | solution.py:40
  52.6 1.8 copy.34
  54.4 1.3 reshape.47
  55.7 2.3 subtract_multiply_fusion
  58.2 65.6 %all-gather.2.cloned.1.call-done = f32[256,3072]{1,0:T(8,128)} async-done(((f32[64,3072]{1,0:T(8,128)}), f32[256,3072]{1,0:T(8,128)}) %all-gather.2.cloned.1.call-update) | async-done | bytes 3145744 | tf_op jit(solution)/shard_map/all_gather | solution.py:49
  123.8 5.9 %fusion.33 = f32[64,256]{1,0:T(8,128)} fusion(f32[64,3072]{1,0:T(8,128)} %subtract_multiply_fusion, f32[256,3072]{1,0:T(8,128)} %all-gather.2.cloned.1.call-done), kind=kOutput, calls=%fused_computation.68 | convolution fusion | flops 603979776 | bytes 3997696 | tf_op jit(solution)/shard_map/dot_general | solution.py:50
  129.7 52.0 %all-reduce.3.cloned.1.call-done = f32[64,256]{1,0:T(8,128)} async-done(((f32[64,256]{1,0:T(8,128)}), f32[64,256]{1,0:T(8,128)}) %all-reduce.3.cloned.1.call-update) | async-done | bytes 65552 | tf_op jit(solution)/shard_map/psum | solution.py:53
  181.7 14.1 %all_gather.7 = f32[256,256]{1,0:T(8,128)S(1)} all-gather(f32[64,256]{1,0:T(8,128)} %all-reduce.3.cloned.1.call-done), channel_id=1, replica_groups=mesh['space'=8,'mode'=4] {'mode'}, dimensions={0}, use_global_device_ids=true | all-gather | bytes 327680 | tf_op jit(solution)/shard_map/all_gather | solution.py:54
  195.9 0.8 copy.35
  196.7 1.0 fusion.13
  198.4 11.7 %cholesky.50 = f32[128,128]{1,0:T(8,128)S(1)} custom-call(f32[128,128]{1,0:T(8,128)S(1)} %cholesky.118), custom_call_target="Cholesky" | custom-call | tf_op jit(solution)/shard_map/jit(cholesky)/cholesky | solution.py:55
  210.8 10.6 %custom-call.15 = f32[1,128,128]{1,2,0:T(8,128)S(1)} custom-call(f32[1,128,128]{2,1,0:T(8,128)} %get-tuple-element.31), custom_call_target="InvertDiagBlocksLowerTriangular" | custom-call | tf_op jit(solution)/shard_map/jit(cholesky)/cholesky | solution.py:55
  221.4 1.0 constant_dynamic-update-slice_fusion
  222.5 1.7 convolution_subtract_fusion.1
  224.2 12.5 %cholesky.105 = f32[128,128]{1,0:T(8,128)S(1)} custom-call(f32[128,128]{1,0:T(8,128)} %convolution_subtract_fusion.1), custom_call_target="Cholesky" | custom-call | tf_op jit(solution)/shard_map/jit(cholesky)/cholesky | solution.py:55
  238.8 1.0 select_select_fusion
  239.8 5.2 %while.1 = (s32[]{:T(128)}, f32[256,256]{1,0:T(8,128)S(1)}, s32[2,2]{1,0:T(2,128)S(1)}, f32[2,128,128]{2,1,0:T(8,128)}, s32[]{:T(128)}) while((s32[]{:T(128)}, f32[256,256]{1,0:T(8,128)S(1)}, s32[2,2]{1,0:T(2,128)S(1)}, f32[2,128,128]{2,1,0:T(8,128)}, s32[]{:T(128)}) %tuple.26), condition=%wide.while_cond, body=%wide.while_body.sunk | while | flops 2 | bytes 132705 | solution.py:57
  240.6 1.9 bitcast_dynamic-update-slice_fusion.2
  243.1 1.9 bitcast_dynamic-update-slice_fusion.2
  245.0 21.1 %custom-call.16 = f32[2,128,128]{1,2,0:T(8,128)} custom-call(f32[2,128,128]{2,1,0:T(8,128)} %get-tuple-element.13), custom_call_target="InvertDiagBlocksLowerTriangular" | custom-call | tf_op jit(solution)/shard_map/jit(_solve_triangular)/triangular_solve | solution.py:57
  266.1 1.1 fusion.14
  267.5 1.2 fusion.20
  268.7 2.9 %fusion.17 = f32[64,3072]{1,0:T(8,128)} fusion(f32[256,3072]{1,0:T(8,128)S(1)} %copy-done, s32[]{:T(128)S(6)} %select_n.15, f32[128,256]{1,0:T(8,128)S(1)} %fusion.14, f32[128,256]{1,0:T(8,128)S(1)} %fusion.20), kind=kOutput, calls=%fused_computation.36 | convolution fusion | flops 603996160 | bytes 4194308 | tf_op jit(solution)/shard_map/dot_general | solution.py:59
  (50 shorter events, 10.1 us)
Async XLA Ops:
  6.5 117.3 %all-gather.2.cloned.1.call-start = ((), (), s32[]{:S(2)}) async-start(), calls=%async_computation | async-start | bytes 3932160 | tf_op jit(solution)/shard_map/all_gather | solution.py:49
  8.4 5.9 %collective-permute-start = (bf16[64,384]{1,0:T(8,128)(2,1)S(1)}, bf16[64,384]{1,0:T(8,128)(2,1)S(1)}, u32[]{:S(2)}, u32[]{:S(2)}) collective-permute-start(bf16[64,384]{1,0:T(8,128)(2,1)S(1)} %get-tuple-element.26), channel_id=1, source_target_pairs={{0,4},{4,8},{8,12},{12,16},{16,20},{20,24},{24,28},{28,0},{1,5},{5... | collective-permute-start | bytes 147464 | tf_op jit(solution)/shard_map/ppermute | solution.py:18
  9.0 5.4 %collective-permute-start.1 = (bf16[64,384]{1,0:T(8,128)(2,1)S(1)}, bf16[64,384]{1,0:T(8,128)(2,1)S(1)}, u32[]{:S(2)}, u32[]{:S(2)}) collective-permute-start(bf16[64,384]{1,0:T(8,128)(2,1)S(1)} %get-tuple-element.27), channel_id=1, source_target_pairs={{4,0},{8,4},{12,8},{16,12},{20,16},{24,20},{28,24},{0,28},{5,1},{9... | collective-permute-start | bytes 147464 | tf_op jit(solution)/shard_map/ppermute | solution.py:20
  29.1 2.3 copy-start.1
  31.5 4.5 %collective-permute-start.2 = (bf16[64,384]{1,0:T(8,128)(2,1)S(1)}, bf16[64,384]{1,0:T(8,128)(2,1)S(1)}, u32[]{:S(2)}, u32[]{:S(2)}) collective-permute-start(bf16[64,384]{1,0:T(8,128)(2,1)S(1)} %get-tuple-element.24), channel_id=1, source_target_pairs={{0,4},{4,8},{8,12},{12,16},{16,20},{20,24},{24,28},{28,0},{1,5},{5... | collective-permute-start | bytes 147464 | tf_op jit(solution)/shard_map/ppermute | solution.py:18
  32.3 3.7 %collective-permute-start.3 = (bf16[64,384]{1,0:T(8,128)(2,1)S(1)}, bf16[64,384]{1,0:T(8,128)(2,1)S(1)}, u32[]{:S(2)}, u32[]{:S(2)}) collective-permute-start(bf16[64,384]{1,0:T(8,128)(2,1)S(1)} %get-tuple-element.25), channel_id=1, source_target_pairs={{4,0},{8,4},{12,8},{16,12},{20,16},{24,20},{28,24},{0,28},{5,1},{9... | collective-permute-start | bytes 147464 | tf_op jit(solution)/shard_map/ppermute | solution.py:20
  58.0 123.8 %all-reduce.3.cloned.1.call-start = ((), (), s32[]{:S(2)}) async-start(), calls=%async_computation.1 | async-start | bytes 131072 | tf_op jit(solution)/shard_map/psum | solution.py:53
  123.8 144.9 %copy-start = (f32[256,3072]{1,0:T(8,128)S(1)}, f32[256,3072]{1,0:T(8,128)}, u32[]{:S(2)}) copy-start(f32[256,3072]{1,0:T(8,128)} %all-gather.2.cloned.1.call-done) | copy-start | bytes 9437188
  197.7 0.7 copy-start.3
  236.8 2.0 copy-start.2
Sparse Core Ops, SparseCore 0:
  58.1 65.6 all-gather.1
  129.8 51.8 all-reduce.2
where the time goes:
time: 279 us; the launch traced here: 278 us
  waiting for transfers between devices  119 us (43%)
  other arithmetic  65.9 us (24%)
  matrix products  36 us (13%)
  local copies, waits for them, and re-layouts  20.9 us (7%)
  between operations  15.5 us (6%)
  blocking collectives  14.1 us (5%)
  starting transfers between devices  6.4 us (2%)
    all_gather x1, waiting for transfers between devices, per_device(): whole = lax.all_gather(second, 'mode', axis=0, tiled=True)  65.6 us
    psum x1, waiting for transfers between devices, per_device(): summed_rows = lax.psum(partial_rows, 'space')  52 us
    another operation x6, other arithmetic, per_device(): lower_factor = jnp.linalg.cholesky(gram)  36.3 us
    another operation x3, other arithmetic, per_device(): jax.scipy.linalg.solve_triangular(lower_factor, identity_matrix, lower=True)  22.1 us
    dot_general x2, matrix products, operate(): jnp.einsum('rkij,prkj->pri', hessian, gathered, preferred_element_type=jn...  22 us
    all_gather x1, blocking collectives, per_device(): gram = lax.all_gather(summed_rows, 'mode', axis=0, tiled=True)  14.1 us
    dot_general x1, matrix products, per_device(): jnp.dot(second, whole.T, precision=lax.Precision.HIGHEST, preferred_eleme...  5.88 us
  transfers between devices with their start and end apart: 6, of which 3 were waited for; matrix products, arithmetic and copies ran while one was open for 1% of the time, Pallas kernels for 0%

commit v1 on v0

--- a/solution.py
+++ b/solution.py
@@ -46,7 +46,15 @@
     image = operate(first.astype(jnp.bfloat16))
     second = (2.0 * (image - filter_center * first) / filter_half - start) * live
     my_index = lax.axis_index("mode")
-    whole = lax.all_gather(second, "mode", axis=0, tiled=True)
+    p_count = jax.lax.axis_size("mode")
+    log = [second]
+    for nth in tuple(range(1, p_count)):
+        n_now = jax.lax.ppermute(
+            log[nth - 1], axis_name="mode", perm=[(d, (d - 1) % p_count) for d in range(p_count)]
+        )
+        log.append(n_now)
+    finding = jnp.concatenate(log, axis=0)
+    whole = jnp.roll(finding, jax.lax.axis_index("mode") * second.shape[0], axis=0)
     partial_rows = jnp.dot(
         second, whole.T, precision=lax.Precision.HIGHEST, preferred_element_type=jnp.float32
     )

time: 279 us -> 271 us (0.971)
  waiting for transfers between devices: 119 us -> 105 us
  starting transfers between devices: 6.4 us -> 19 us
  other arithmetic: 65.9 us -> 59.6 us
  local copies, waits for them, and re-layouts: 20.9 us -> 23.8 us
    all_gather x1 -> x0, waiting for transfers between devices: 65.6 us -> none  [per_device(): whole = lax.all_gather(second, 'mode', axis=0, tiled=True)]
    ppermute x0 -> x3, waiting for transfers between devices: none -> 47.6 us  [per_device(): jax.lax.ppermute(log[nth - 1], axis_name='mode', perm=[(d, (d - 1) % p_co...]
    ppermute x0 -> x3, starting transfers between devices: none -> 12.9 us  [per_device(): jax.lax.ppermute(log[nth - 1], axis_name='mode', perm=[(d, (d - 1) % p_co...]
    unnamed x8, local copies, waits for them, and re-layouts: 0.71 us -> 5.66 us
    psum x1, waiting for transfers between devices: 52 us -> 55.2 us  [per_device(): summed_rows = lax.psum(partial_rows, 'space')]
  transfers between devices with their start and end apart: 6 -> 8, of which waited for: 3 -> 5; matrix products, arithmetic and copies ran while one was open for 1% -> 2% of each run, Pallas kernels for 0% -> 0%
where the time goes in v1:
time: 271 us; the launch traced here: 270 us
  waiting for transfers between devices  105 us (39%)
  other arithmetic  59.6 us (22%)
  matrix products  33.6 us (12%)
  local copies, waits for them, and re-layouts  23.8 us (9%)
  starting transfers between devices  19 us (7%)
  between operations  15.6 us (6%)
  blocking collectives  14.1 us (5%)
    psum x1, waiting for transfers between devices, per_device(): summed_rows = lax.psum(partial_rows, 'space')  55.2 us
    ppermute x3, waiting for transfers between devices, per_device(): jax.lax.ppermute(log[nth - 1], axis_name='mode', perm=[(d, (d - 1) % p_co...  47.6 us
    another operation x6, other arithmetic, per_device(): lower_factor = jnp.linalg.cholesky(gram)  34 us
    dot_general x2, matrix products, operate(): jnp.einsum('rkij,prkj->pri', hessian, gathered, preferred_element_type=jn...  22 us
    another operation x3, other arithmetic, per_device(): jax.scipy.linalg.solve_triangular(lower_factor, identity_matrix, lower=True)  19.7 us
    all_gather x1, blocking collectives, per_device(): gram = lax.all_gather(summed_rows, 'mode', axis=0, tiled=True)  14.1 us
    ppermute x3, starting transfers between devices, per_device(): jax.lax.ppermute(log[nth - 1], axis_name='mode', perm=[(d, (d - 1) % p_co...  12.9 us
    unnamed x8, local copies, waits for them, and re-layouts  5.66 us
  transfers between devices with their start and end apart: 8, of which 5 were waited for; matrix products, arithmetic and copies ran while one was open for 2% of the time, Pallas kernels for 0%

profile of v1, /device:TPU:0, one launch (start us, length us, event | category | flops | bytes accessed | tf_op | source)
XLA Modules:
  0.0 270.4 jit_solution(17662306568042413350)
XLA Ops:
  7.2 1.2 multiply_convert_fusion
  9.0 2.9 %collective-permute-start.1 = (bf16[64,384]{1,0:T(8,128)(2,1)S(1)}, bf16[64,384]{1,0:T(8,128)(2,1)S(1)}, u32[]{:S(2)}, u32[]{:S(2)}) collective-permute-start(bf16[64,384]{1,0:T(8,128)(2,1)S(1)} %get-tuple-element.29), channel_id=1, source_target_pairs={{4,0},{8,4},{12,8},{16,12},{20,16},{24,20},{28,24},{0,28},{5,1},{9... | collective-permute-start | bytes 147464 | tf_op jit(solution)/shard_map/ppermute | solution.py:20
  15.3 2.7 %gather_fusion = bf16[128,64,192]{2,1,0:T(8,128)(2,1)} fusion(bf16[64,20,192]{2,0,1:T(8,128)(2,1)S(1)} %copy.29, s32[1024]{0:T(1024)S(1)} %pad_clamp_fusion), kind=kCustom, calls=%fused_computation.clone | custom fusion | bytes 6291968 | tf_op jit(solution)/shard_map/jit(_take)/gather | solution.py:38
  18.1 11.0 %fusion.14 = f32[64,16,192]{2,0,1:T(8,128)} fusion(bf16[16,8,192,192]{3,2,1,0:T(8,128)(2,1)} %param.8, bf16[16,8,64,192]{3,2,1,0:T(8,128)(2,1)} %bitcast.58, pred[16,8]{1,0:T(8,128)(4,1)S(1)} %copy.26, bf16[16,8]{1,0:T(8,128)(2,1)S(1)} %copy.30), kind=kOutput, calls=%fused_computation.20 | convolution fusion | flops 607125504 | bytes 13369728 | tf_op jit(solution)/shard_map/rkij,prkj->pri/dot_general | solution.py:40
  29.1 1.8 copy.31
  32.3 1.9 collective-permute-start.3
  34.2 1.8 collective-permute-done.2
  37.0 2.7 %gather_fusion.1 = bf16[128,64,192]{2,1,0:T(8,128)(2,1)} fusion(bf16[64,20,192]{2,0,1:T(8,128)(2,1)S(1)} %copy.33, s32[1024]{0:T(1024)S(1)} %pad_clamp_fusion), kind=kCustom, calls=%fused_computation.1.clone | custom fusion | bytes 6291968 | tf_op jit(solution)/shard_map/jit(_take)/gather | solution.py:38
  39.7 11.0 %fusion.15 = f32[64,16,192]{2,0,1:T(8,128)} fusion(bf16[16,8,192,192]{3,2,1,0:T(8,128)(2,1)} %param.8, bf16[16,8,64,192]{3,2,1,0:T(8,128)(2,1)} %bitcast.57, pred[16,8]{1,0:T(8,128)(4,1)S(1)} %copy.26, bf16[16,8]{1,0:T(8,128)(2,1)S(1)} %copy.30), kind=kOutput, calls=%fused_computation.21 | convolution fusion | flops 607125504 | bytes 13369728 | tf_op jit(solution)/shard_map/rkij,prkj->pri/dot_general | solution.py:40
  50.7 1.8 copy.34
  52.5 1.3 reshape.47
  53.8 2.3 constant_dynamic-update-slice_fusion.7
  56.1 4.3 %collective-permute-start.4 = (f32[64,3072]{1,0:T(8,128)S(1)}, f32[64,3072]{1,0:T(8,128)S(1)}, u32[]{:S(2)}, u32[]{:S(2)}) collective-permute-start(f32[64,3072]{1,0:T(8,128)S(1)} %get-tuple-element.23), channel_id=1, source_target_pairs={{0,3},{1,0},{2,1},{3,2},{4,7},{5,4},{6,5},{7,6},{8,11},{9,8},{10,9... | collective-permute-start | bytes 2359304 | tf_op jit(solution)/shard_map/ppermute | solution.py:52
  60.4 17.4 %collective-permute-done.4 = f32[64,3072]{1,0:T(8,128)S(1)} collective-permute-done((f32[64,3072]{1,0:T(8,128)S(1)}, f32[64,3072]{1,0:T(8,128)S(1)}, u32[]{:S(2)}, u32[]{:S(2)}) %collective-permute-start.4) | collective-permute-done | bytes 786464 | tf_op jit(solution)/shard_map/ppermute | solution.py:52
  77.8 4.3 %collective-permute-start.5 = (f32[64,3072]{1,0:T(8,128)S(1)}, f32[64,3072]{1,0:T(8,128)S(1)}, u32[]{:S(2)}, u32[]{:S(2)}) collective-permute-start(f32[64,3072]{1,0:T(8,128)S(1)} %collective-permute-done.4), channel_id=1, source_target_pairs={{0,3},{1,0},{2,1},{3,2},{4,7},{5,4},{6,5},{7,6},{8,11},{9,8},{10,9... | collective-permute-start | bytes 2359304 | tf_op jit(solution)/shard_map/ppermute | solution.py:52
  82.1 16.5 %collective-permute-done.5 = f32[64,3072]{1,0:T(8,128)S(1)} collective-permute-done((f32[64,3072]{1,0:T(8,128)S(1)}, f32[64,3072]{1,0:T(8,128)S(1)}, u32[]{:S(2)}, u32[]{:S(2)}) %collective-permute-start.5) | collective-permute-done | bytes 786464 | tf_op jit(solution)/shard_map/ppermute | solution.py:52
  98.6 4.3 %collective-permute-start.6 = (f32[64,3072]{1,0:T(8,128)S(1)}, f32[64,3072]{1,0:T(8,128)S(1)}, u32[]{:S(2)}, u32[]{:S(2)}) collective-permute-start(f32[64,3072]{1,0:T(8,128)S(1)} %collective-permute-done.5), channel_id=1, source_target_pairs={{0,3},{1,0},{2,1},{3,2},{4,7},{5,4},{6,5},{7,6},{8,11},{9,8},{10,9... | collective-permute-start | bytes 2359304 | tf_op jit(solution)/shard_map/ppermute | solution.py:52
  103.8 0.9 constant_dynamic-update-slice_fusion.5
  104.8 13.7 %collective-permute-done.6 = f32[64,3072]{1,0:T(8,128)S(1)} collective-permute-done((f32[64,3072]{1,0:T(8,128)S(1)}, f32[64,3072]{1,0:T(8,128)S(1)}, u32[]{:S(2)}, u32[]{:S(2)}) %collective-permute-start.6) | collective-permute-done | bytes 786464 | tf_op jit(solution)/shard_map/ppermute | solution.py:52
  120.4 0.9 constant_dynamic-update-slice_fusion.2
  121.3 1.0 constant_dynamic-update-slice_fusion.1
  123.2 5.5 %fusion.8 = f32[64,256]{1,0:T(8,128)} fusion(f32[64,3072]{1,0:T(8,128)S(1)} %get-tuple-element.23, f32[512,3072]{1,0:T(8,128)} %constant_dynamic-update-slice_fusion, s32[]{:T(128)S(6)} %select_n.28), kind=kOutput, calls=%fused_computation.14 | convolution fusion | flops 603979776 | bytes 3997700 | tf_op jit(solution)/shard_map/dot_general | solution.py:58
  128.8 55.2 %all-reduce.3.cloned.1.call-done = f32[64,256]{1,0:T(8,128)} async-done(((f32[64,256]{1,0:T(8,128)}), f32[64,256]{1,0:T(8,128)}) %all-reduce.3.cloned.1.call-update) | async-done | bytes 65552 | tf_op jit(solution)/shard_map/psum | solution.py:61
  183.9 14.1 %all_gather.3 = f32[256,256]{1,0:T(8,128)S(1)} all-gather(f32[64,256]{1,0:T(8,128)} %all-reduce.3.cloned.1.call-done), channel_id=1, replica_groups=mesh['space'=8,'mode'=4] {'mode'}, dimensions={0}, use_global_device_ids=true | all-gather | bytes 327680 | tf_op jit(solution)/shard_map/all_gather | solution.py:62
  198.3 11.7 %cholesky.50 = f32[128,128]{1,0:T(8,128)S(1)} custom-call(f32[128,128]{1,0:T(8,128)S(1)} %cholesky.118), custom_call_target="Cholesky" | custom-call | tf_op jit(solution)/shard_map/jit(cholesky)/cholesky | solution.py:63
  210.0 9.8 %custom-call.15 = f32[1,128,128]{1,2,0:T(8,128)S(1)} custom-call(f32[1,128,128]{2,1,0:T(8,128)S(1)} %get-tuple-element.33), custom_call_target="InvertDiagBlocksLowerTriangular" | custom-call | tf_op jit(solution)/shard_map/jit(cholesky)/cholesky | solution.py:63
  220.3 11.7 %cholesky.105 = f32[128,128]{1,0:T(8,128)S(1)} custom-call(f32[128,128]{1,0:T(8,128)S(1)} %convolution_subtract_fusion.1), custom_call_target="Cholesky" | custom-call | tf_op jit(solution)/shard_map/jit(cholesky)/cholesky | solution.py:63
  234.2 4.1 %while.1 = (s32[]{:T(128)}, f32[256,256]{1,0:T(8,128)S(1)}, s32[2,2]{1,0:T(2,128)S(1)}, f32[2,128,128]{2,1,0:T(8,128)S(1)}, s32[]{:T(128)}) while((s32[]{:T(128)}, f32[256,256]{1,0:T(8,128)S(1)}, s32[2,2]{1,0:T(2,128)S(1)}, f32[2,128,128]{2,1,0:T(8,128)S(1)}, s32[]{:T(128)}) %tuple.27), condition=%wide.while_cond, body=%wide.while_body.sunk | while | flops 2 | bytes 131181 | solution.py:65
  234.9 1.4 bitcast_dynamic-update-slice_fusion.2
  236.9 1.4 bitcast_dynamic-update-slice_fusion.2
  238.3 19.7 %custom-call.16 = f32[2,128,128]{1,2,0:T(8,128)S(1)} custom-call(f32[2,128,128]{2,1,0:T(8,128)S(1)} %get-tuple-element.13), custom_call_target="InvertDiagBlocksLowerTriangular" | custom-call | tf_op jit(solution)/shard_map/jit(_solve_triangular)/triangular_solve | solution.py:65
  258.8 4.8 %fusion.6 = f32[64,3072]{1,0:T(8,128)} fusion(f32[512,3072]{1,0:T(8,128)} %constant_dynamic-update-slice_fusion, s32[]{:T(128)S(6)} %select_n.28, s32[]{:T(128)S(6)} %select_n.30, f32[128,256]{1,0:T(8,128)S(1)} %fusion.18, f32[128,256]{1,0:T(8,128)S(1)} %fusion.23), kind=kOutput, calls=%fused_computation.12 | convolution fusion | flops 603996160 | bytes 4194312 | tf_op jit(solution)/shard_map/dot_general | solution.py:67
  (54 shorter events, 13.6 us)
Async XLA Ops:
  6.5 177.4 %all-reduce.3.cloned.1.call-start = ((), (), s32[]{:S(2)}) async-start(), calls=%async_computation | async-start | bytes 131072 | tf_op jit(solution)/shard_map/psum | solution.py:61
  8.4 5.9 %collective-permute-start = (bf16[64,384]{1,0:T(8,128)(2,1)S(1)}, bf16[64,384]{1,0:T(8,128)(2,1)S(1)}, u32[]{:S(2)}, u32[]{:S(2)}) collective-permute-start(bf16[64,384]{1,0:T(8,128)(2,1)S(1)} %get-tuple-element.28), channel_id=1, source_target_pairs={{0,4},{4,8},{8,12},{12,16},{16,20},{20,24},{24,28},{28,0},{1,5},{5... | collective-permute-start | bytes 147464 | tf_op jit(solution)/shard_map/ppermute | solution.py:18
  9.0 5.4 %collective-permute-start.1 = (bf16[64,384]{1,0:T(8,128)(2,1)S(1)}, bf16[64,384]{1,0:T(8,128)(2,1)S(1)}, u32[]{:S(2)}, u32[]{:S(2)}) collective-permute-start(bf16[64,384]{1,0:T(8,128)(2,1)S(1)} %get-tuple-element.29), channel_id=1, source_target_pairs={{4,0},{8,4},{12,8},{16,12},{20,16},{24,20},{28,24},{0,28},{5,1},{9... | collective-permute-start | bytes 147464 | tf_op jit(solution)/shard_map/ppermute | solution.py:20
  18.1 13.3 %copy-start = (f32[64,3072]{1,0:T(8,128)S(1)}, f32[64,3072]{1,0:T(8,128)}, u32[]{:S(2)}) copy-start(f32[64,3072]{1,0:T(8,128)} %param.7) | copy-start | bytes 2359300
  31.5 4.5 %collective-permute-start.2 = (bf16[64,384]{1,0:T(8,128)(2,1)S(1)}, bf16[64,384]{1,0:T(8,128)(2,1)S(1)}, u32[]{:S(2)}, u32[]{:S(2)}) collective-permute-start(bf16[64,384]{1,0:T(8,128)(2,1)S(1)} %get-tuple-element.26), channel_id=1, source_target_pairs={{0,4},{4,8},{8,12},{12,16},{16,20},{20,24},{24,28},{28,0},{1,5},{5... | collective-permute-start | bytes 147464 | tf_op jit(solution)/shard_map/ppermute | solution.py:18
  32.3 3.7 %collective-permute-start.3 = (bf16[64,384]{1,0:T(8,128)(2,1)S(1)}, bf16[64,384]{1,0:T(8,128)(2,1)S(1)}, u32[]{:S(2)}, u32[]{:S(2)}) collective-permute-start(bf16[64,384]{1,0:T(8,128)(2,1)S(1)} %get-tuple-element.27), channel_id=1, source_target_pairs={{4,0},{8,4},{12,8},{16,12},{20,16},{24,20},{28,24},{0,28},{5,1},{9... | collective-permute-start | bytes 147464 | tf_op jit(solution)/shard_map/ppermute | solution.py:20
  56.1 21.7 %collective-permute-start.4 = (f32[64,3072]{1,0:T(8,128)S(1)}, f32[64,3072]{1,0:T(8,128)S(1)}, u32[]{:S(2)}, u32[]{:S(2)}) collective-permute-start(f32[64,3072]{1,0:T(8,128)S(1)} %get-tuple-element.23), channel_id=1, source_target_pairs={{0,3},{1,0},{2,1},{3,2},{4,7},{5,4},{6,5},{7,6},{8,11},{9,8},{10,9... | collective-permute-start | bytes 2359304 | tf_op jit(solution)/shard_map/ppermute | solution.py:52
  77.8 20.8 %collective-permute-start.5 = (f32[64,3072]{1,0:T(8,128)S(1)}, f32[64,3072]{1,0:T(8,128)S(1)}, u32[]{:S(2)}, u32[]{:S(2)}) collective-permute-start(f32[64,3072]{1,0:T(8,128)S(1)} %collective-permute-done.4), channel_id=1, source_target_pairs={{0,3},{1,0},{2,1},{3,2},{4,7},{5,4},{6,5},{7,6},{8,11},{9,8},{10,9... | collective-permute-start | bytes 2359304 | tf_op jit(solution)/shard_map/ppermute | solution.py:52
  98.6 19.9 %collective-permute-start.6 = (f32[64,3072]{1,0:T(8,128)S(1)}, f32[64,3072]{1,0:T(8,128)S(1)}, u32[]{:S(2)}, u32[]{:S(2)}) collective-permute-start(f32[64,3072]{1,0:T(8,128)S(1)} %collective-permute-done.5), channel_id=1, source_target_pairs={{0,3},{1,0},{2,1},{3,2},{4,7},{5,4},{6,5},{7,6},{8,11},{9,8},{10,9... | collective-permute-start | bytes 2359304 | tf_op jit(solution)/shard_map/ppermute | solution.py:52
Sparse Core Ops, SparseCore 0:
  128.9 55.0 all-reduce.2
